TPU v7x, 256 devices: a whole 4x4x8 slice. The times are simulated.
256 devices in a mesh: row: 32 (over y, z), col: 8 (over x, core).
Axes of the slice: x: 4, y: 4, z: 8, core: 2. Of those that a mesh axis runs over, the one named last changes fastest.
Arguments:
- blocks: bfloat16 [4096, 3, 128, 128], P(('row', 'col')), may hold values from -0.3984375 to 0.3984375
- rows: int32 [4096, 3], P(('row', 'col')), may hold values from 0 to 63, as said below
- counts: int32 [4096], P(('row', 'col')), may hold values from 1 to 3
- sketch: bfloat16 [524288, 128], P(('row', 'col')), may hold values from -6 to 6
- weights: float32 [8192], replicated, may hold values from 0.35 to 2.8
Outputs:
- basis_out: float32 [8192, 128], P(('row', 'col'))
- right_factors: bfloat16 [524288, 128], P(('row', 'col'))
Inputs may be any that keep to these rules, and one draw needn't show every extreme that they name: `rows`: the 3 entries of each document block are distinct feature blocks.
All inputs are finite; a program needn't handle non-finite values.
Results may differ from a plain program's by a relative error of at most 0.0049.
Values may be sent and summed in bfloat16 or wider, within the bound.
A program may use at most 64 MiB of HBM per device.

v0:
```python
import jax
import jax.numpy as jnp
from jax import lax
from jax.sharding import PartitionSpec as P

HIGHEST = lax.Precision.HIGHEST


def body(blocks, rows, counts, sketch, weights):
    doc_blocks = blocks.shape[0]
    slot_count = blocks.shape[1]
    block_width = blocks.shape[2]
    columns = sketch.shape[1]
    features = weights.shape[0]
    feature_blocks = features // block_width
    in_use = lax.broadcasted_iota(jnp.int32, (doc_blocks, slot_count), 1) < counts[:, None]
    segment_ids = jnp.where(in_use, rows, feature_blocks).reshape(-1)
    row_count = lax.axis_size("row")
    col_count = lax.axis_size("col")
    flat_rows = features // (row_count * col_count)
    flat_index = lax.axis_index("row") * col_count + lax.axis_index("col")
    flat_start = flat_index * flat_rows
    flat_weights = lax.dynamic_slice_in_dim(weights, flat_start, flat_rows)[:, None]
    width_now = sketch.shape[1]
    tiles_docs = sketch.reshape(doc_blocks, block_width, width_now)
    terms = jnp.einsum("dsfk,dkl->dsfl", blocks, tiles_docs, preferred_element_type=jnp.float32)
    terms = terms.reshape(doc_blocks * slot_count, block_width, width_now)
    summed = jax.ops.segment_sum(terms, segment_ids, num_segments=feature_blocks + 1)
    local_terms = summed[:feature_blocks].reshape(features, sketch.shape[1])
    flat_summed = (
        lax.psum_scatter(local_terms, ("row", "col"), scatter_dimension=0, tiled=True)
        * flat_weights
    )
    chol_factor = jnp.linalg.cholesky(
        lax.psum(jnp.dot(flat_summed.T, flat_summed, precision=HIGHEST), ("row", "col")) / features
    )
    inverse = jax.scipy.linalg.solve_triangular(
        chol_factor, jnp.eye(columns, dtype=jnp.float32), lower=True
    )
    current = jnp.dot(flat_summed, inverse.T, precision=HIGHEST)
    weighted = (current * flat_weights).astype(jnp.bfloat16)
    gathered = lax.all_gather(weighted, ("row", "col"), axis=0, tiled=True)
    width_now = gathered.shape[1]
    picked = gathered.reshape(feature_blocks, block_width, width_now)[rows]
    picked = jnp.where(in_use[:, :, None, None], picked, jnp.zeros((), gathered.dtype))
    product = jnp.einsum("dsfl,dsfk->dkl", picked, blocks, preferred_element_type=jnp.float32)
    factors = product.reshape(doc_blocks * block_width, width_now).astype(jnp.bfloat16)
    return (current, factors)


def solution(mesh):
    placed = (
        P(("row", "col"), None, None, None),
        P(("row", "col"), None),
        P(("row", "col")),
        P(("row", "col"), None),
        P(),
    )
    return jax.shard_map(
        body,
        mesh=mesh,
        in_specs=placed,
        out_specs=(P(("row", "col"), None), P(("row", "col"), None)),
        check_vma=False,
    )
```

profile of v0, /device:TPU:1, one launch (start us, length us, event | category | flops | bytes accessed | tf_op | source)
XLA Modules:
  0.0 1698.7 jit_solution(12156809714150162819)
XLA Ops:
  7.2 0.0 copy-start
  7.2 0.0 reduce-scatter.2.cloned.1.call-start
  7.2 0.8 compare_select_fusion
  8.0 0.1 copy.13
  8.1 0.1 reshape.61
  8.2 0.4 copy-done
  8.6 3.3 fusion.21
  11.9 2.5 broadcast_in_dim.27
  14.4 10.1 scatter_fusion
  24.5 4.7 slice.18
  29.2 0.0 copy-start.1
  29.2 0.0 reduce-scatter.2.cloned.1.call-update
  29.2 0.0 all-reduce.2.cloned.1.call-start
  29.2 0.8 dynamic_slice.3
  30.0 1285.1 %reduce-scatter.2.cloned.1.call-done = f32[32,128]{1,0:T(8,128)} async-done(((f32[8192,128]{1,0:T(8,128)}), f32[32,128]{1,0:T(8,128)}) %reduce-scatter.2.cloned.1.call-update) | async-done | bytes 16400 | tf_op jit(solution)/shard_map/reduce_scatter | solution.py:31
  1315.1 1.8 fusion.16
  1316.9 0.0 all-reduce.2.cloned.1.call-update
  1316.9 0.0 all-gather.2.cloned.1.call-start
  1317.0 243.9 %all-reduce.2.cloned.1.call-done = f32[128,128]{0,1:T(8,128)} async-done(((f32[128,128]{0,1:T(8,128)}), f32[128,128]{0,1:T(8,128)}) %all-reduce.2.cloned.1.call-update) | async-done | bytes 65552 | tf_op jit(solution)/shard_map/psum | solution.py:35
  1560.9 0.8 broadcast_multiply_fusion
  1561.7 0.1 copy.15
  1561.8 0.9 fusion.13
  1562.7 11.7 cholesky.17
  1574.4 0.6 compare_reduce_fusion
  1575.1 0.7 fusion.10
  1575.7 9.8 custom-call.7
  1585.5 0.2 fusion.11
  1585.8 1.6 multiply_convert_fusion
  1587.4 0.0 all-gather.2.cloned.1.call-update
  1587.4 0.1 copy.17
  1587.5 0.1 reshape.53
  1587.6 0.0 copy-done.1
  1587.6 0.1 copy.16
  1587.7 100.5 %all-gather.2.cloned.1.call-done = bf16[8192,128]{1,0:T(8,128)(2,1)} async-done(((bf16[32,128]{1,0:T(8,128)(2,1)}), bf16[8192,128]{1,0:T(8,128)(2,1)}) %all-gather.2.cloned.1.call-update) | async-done | bytes 2097168 | tf_op jit(solution)/shard_map/all_gather | solution.py:42
  1688.2 2.4 gather_fusion
  1690.7 1.5 fusion.6
  (3 shorter events, 0.0 us)
Async XLA Ops:
  7.2 1.4 copy-start
  7.2 1308.0 %reduce-scatter.2.cloned.1.call-start = ((), (), s32[]{:S(2)}) async-start(), calls=%async_computation.1 | async-start | bytes 4210688 | tf_op jit(solution)/shard_map/reduce_scatter | solution.py:31
  29.2 1558.4 %copy-start.1 = (s32[16]{0:T(128)S(1)}, s32[16]{0:T(128)}, u32[]{:S(2)}) copy-start(s32[16]{0:T(128)} %param.7) | copy-start | bytes 196
  29.2 1531.7 %all-reduce.2.cloned.1.call-start = ((), (), s32[]{:S(2)}) async-start(), calls=%async_computation.2 | async-start | bytes 131072 | tf_op jit(solution)/shard_map/psum | solution.py:35
  1316.9 371.3 %all-gather.2.cloned.1.call-start = ((), (), s32[]{:S(2)}) async-start(), calls=%async_computation.3 | async-start | bytes 2105344 | tf_op jit(solution)/shard_map/all_gather | solution.py:42
Sparse Core Ops, SparseCore 0:
  29.3 1285.7 reduce-scatter.1
  1321.2 239.5 all-reduce.1
  1587.5 100.6 all-gather.1
where the time goes:
time: 1700 us
  waiting for transfers between devices  1630 us (96%)
  other arithmetic  35.5 us (2%)
    reduce_scatter x1, waiting for transfers between devices, body(): lax.psum_scatter(local_terms, ('row', 'col'), scatter_dimension=0, tiled=...  1290 us
    psum x1, waiting for transfers between devices, body(): lax.psum(jnp.dot(flat_summed.T, flat_summed, precision=HIGHEST), ('row',...  244 us
    all_gather x1, waiting for transfers between devices, body(): gathered = lax.all_gather(weighted, ('row', 'col'), axis=0, tiled=True)  101 us
  transfers between devices with their start and end apart: 3, of which 3 were waited for; matrix products, arithmetic and copies ran while one was open for 0% of the time, Pallas kernels for 0%

commit v1 on v0

--- a/solution.py
+++ b/solution.py
@@ -32,7 +32,10 @@
         * flat_weights
     )
     chol_factor = jnp.linalg.cholesky(
-        lax.psum(jnp.dot(flat_summed.T, flat_summed, precision=HIGHEST), ("row", "col")) / features
+        jax.lax.psum(
+            jax.lax.psum(jnp.dot(flat_summed.T, flat_summed, precision=HIGHEST), "col"), "row"
+        )
+        / features
     )
     inverse = jax.scipy.linalg.solve_triangular(
         chol_factor, jnp.eye(columns, dtype=jnp.float32), lower=True

time: 1700 us -> 1670 us (0.982)
  waiting for transfers between devices: 1630 us -> 1600 us
    psum x1 -> x2, waiting for transfers between devices: 244 us -> 203 us  [the longest x1 141 us: body(): jax.lax.psum(jax.lax.psum(jnp.dot(flat_summed.T, flat_summed, precision=H...]
  transfers between devices with their start and end apart: 3 -> 4, of which waited for: 3 -> 4; matrix products, arithmetic and copies ran while one was open for 0% -> 0% of each run, Pallas kernels for 0% -> 0%
where the time goes in v1:
time: 1670 us; the launch traced here: 1660 us
  waiting for transfers between devices  1600 us (96%)
  other arithmetic  35.5 us (2%)
    reduce_scatter x1, waiting for transfers between devices, body(): lax.psum_scatter(local_terms, ('row', 'col'), scatter_dimension=0, tiled=...  1290 us
    psum x1, waiting for transfers between devices, body(): jax.lax.psum(jax.lax.psum(jnp.dot(flat_summed.T, flat_summed, precision=H...  141 us
    all_gather x1, waiting for transfers between devices, body(): gathered = lax.all_gather(weighted, ('row', 'col'), axis=0, tiled=True)  107 us
    psum x1, waiting for transfers between devices, body(): jax.lax.psum(jnp.dot(flat_summed.T, flat_summed, precision=HIGHEST), 'col')  61.7 us
  transfers between devices with their start and end apart: 4, of which 4 were waited for; matrix products, arithmetic and copies ran while one was open for 0% of the time, Pallas kernels for 0%

profile of v1, /device:TPU:1, one launch (start us, length us, event | category | flops | bytes accessed | tf_op | source)
XLA Modules:
  0.0 1664.4 jit_solution(5926269524902462967)
XLA Ops:
  7.2 0.0 copy-start
  7.2 0.0 reduce-scatter.2.cloned.1.call-start
  7.2 0.8 compare_select_fusion
  8.0 0.1 copy.13
  8.1 0.1 reshape.61
  8.2 0.4 copy-done
  8.6 3.3 fusion.21
  11.9 2.5 broadcast_in_dim.27
  14.4 10.1 scatter_fusion
  24.5 4.7 slice.18
  29.2 0.0 copy-start.1
  29.2 0.0 reduce-scatter.2.cloned.1.call-update
  29.2 0.0 all-reduce.3.cloned.1.call-start
  29.2 0.8 dynamic_slice.3
  30.0 1285.1 %reduce-scatter.2.cloned.1.call-done = f32[32,128]{1,0:T(8,128)} async-done(((f32[8192,128]{1,0:T(8,128)}), f32[32,128]{1,0:T(8,128)}) %reduce-scatter.2.cloned.1.call-update) | async-done | bytes 16400 | tf_op jit(solution)/shard_map/reduce_scatter | solution.py:31
  1315.1 1.8 fusion.16
  1316.9 0.0 all-reduce.3.cloned.1.call-update
  1316.9 0.0 all-reduce.5.cloned.1.call-start
  1317.0 61.7 %all-reduce.3.cloned.1.call-done = f32[128,128]{0,1:T(8,128)} async-done(((f32[128,128]{0,1:T(8,128)}), f32[128,128]{0,1:T(8,128)}) %all-reduce.3.cloned.1.call-update) | async-done | bytes 65552 | tf_op jit(solution)/shard_map/psum | solution.py:36
  1378.7 0.0 all-reduce.5.cloned.1.call-update
  1378.7 0.0 all-gather.2.cloned.1.call-start
  1378.7 141.5 %all-reduce.5.cloned.1.call-done = f32[128,128]{0,1:T(8,128)} async-done(((f32[128,128]{0,1:T(8,128)}), f32[128,128]{0,1:T(8,128)}) %all-reduce.5.cloned.1.call-update) | async-done | bytes 65552 | tf_op jit(solution)/shard_map/psum | solution.py:35
  1520.2 0.8 broadcast_multiply_fusion
  1521.1 0.1 copy.15
  1521.2 0.9 fusion.13
  1522.0 11.7 cholesky.17
  1533.8 0.6 compare_reduce_fusion
  1534.4 0.7 fusion.10
  1535.1 9.8 custom-call.7
  1544.9 0.2 fusion.11
  1545.1 1.6 multiply_convert_fusion
  1546.7 0.0 all-gather.2.cloned.1.call-update
  1546.7 0.1 copy.17
  1546.8 0.1 reshape.53
  1546.9 0.0 copy-done.1
  1546.9 0.1 copy.16
  1547.0 106.9 %all-gather.2.cloned.1.call-done = bf16[8192,128]{1,0:T(8,128)(2,1)} async-done(((bf16[32,128]{1,0:T(8,128)(2,1)}), bf16[8192,128]{1,0:T(8,128)(2,1)}) %all-gather.2.cloned.1.call-update) | async-done | bytes 2097168 | tf_op jit(solution)/shard_map/all_gather | solution.py:45
  1653.9 2.4 gather_fusion
  1656.4 1.5 fusion.6
  (3 shorter events, 0.0 us)
Async XLA Ops:
  7.2 1.4 copy-start
  7.2 1308.0 %reduce-scatter.2.cloned.1.call-start = ((), (), s32[]{:S(2)}) async-start(), calls=%async_computation.1 | async-start | bytes 4210688 | tf_op jit(solution)/shard_map/reduce_scatter | solution.py:31
  29.2 1517.8 %copy-start.1 = (s32[16]{0:T(128)S(1)}, s32[16]{0:T(128)}, u32[]{:S(2)}) copy-start(s32[16]{0:T(128)} %param.7) | copy-start | bytes 196
  29.2 1349.5 %all-reduce.3.cloned.1.call-start = ((), (), s32[]{:S(2)}) async-start(), calls=%async_computation.2 | async-start | bytes 131072 | tf_op jit(solution)/shard_map/psum | solution.py:36
  1316.9 203.3 %all-reduce.5.cloned.1.call-start = ((), (), s32[]{:S(2)}) async-start(), calls=%async_computation.3 | async-start | bytes 131072 | tf_op jit(solution)/shard_map/psum | solution.py:35
  1378.7 275.2 %all-gather.2.cloned.1.call-start = ((), (), s32[]{:S(2)}) async-start(), calls=%async_computation.4 | async-start | bytes 2105344 | tf_op jit(solution)/shard_map/all_gather | solution.py:45
Sparse Core Ops, SparseCore 0:
  29.3 1285.7 reduce-scatter.1
  1318.0 60.6 all-reduce.2
  1382.1 138.0 all-reduce.4
  1546.9 107.0 all-gather.1
